TPU v7x, 256 devices: a whole 4x4x8 slice. The times are simulated.
256 devices in a mesh: start: 2 (over core), pencil: 128 (over z, x, y).
Axes of the slice: x: 4, y: 4, z: 8, core: 2. Of those that a mesh axis runs over, the one named last changes fastest.
Arguments:
- template: bfloat16 [512, 64, 512], P('pencil', 'start'), parts along dimension 1, may hold values from -3.5 to 3.5
- reference_image: bfloat16 [512, 64, 512], P('pencil', 'start'), parts along dimension 1, may hold values from -3.5 to 3.5
- velocity: float32 [6, 512, 32, 512], P('start', 'pencil'), parts along dimension 0, may hold values from -4 to 4
- dep_owner: int32 [4, 32768], P('start', 'pencil'), parts along dimension 0, may hold values from 0 to 127, as said below
- dep_offset: int32 [4, 32768], P('start', 'pencil'), parts along dimension 0, may hold values from 0 to 255
- dep_weight: int32 [4, 32768], P('start', 'pencil'), parts along dimension 0, may hold values from 0 to 15
Outputs:
- warped: bfloat16 [512, 64, 512], P('pencil', 'start'), parts along dimension 1
- gradient: float32 [6, 512, 32, 512], P('start', 'pencil'), parts along dimension 0
There are 2 independent parts, one for each index of `start`. A program takes and returns all parts, laid end to end along the dimension named above; each array names one. Nothing has to cross between parts.
Inputs may be any that keep to these rules, and one draw needn't show every extreme that they name: Device d holds blocks d * 256 to (d + 1) * 256 - 1. For a block of device d, dep_owner is (d + m) mod 128 with m one of -2, -1, 0, 1, so that its stencil rows lie on devices d - 2 to d + 2 (modulo 128).
All inputs are finite; a program needn't handle non-finite values.
Results may differ from a plain program's by a relative error of at most 0.012.
Values may be sent and summed in bfloat16 or wider, within the bound.
No kernel may reach another device: no remote copies, remote signals or barrier semaphores. Data moves between devices by JAX's collectives and lax.ppermute only.
A program may use at most 192 MiB of HBM per device.

v0:
```python
import math
import jax
import jax.numpy as jnp
from jax import lax
from jax.sharding import PartitionSpec as P

ZB = 2
SEG = 128
Q = 16
h1_weight = 64.0
force_gain = 32.0


def shifted(x, axis, by):
    length = lax.axis_size(axis)
    return lax.ppermute(x, axis, [(i, (i + by) % length) for i in range(length)])


def dft_tables(length):
    series = jnp.arange(length, dtype=jnp.int32)
    product = series[:, None] * series[None, :] % length
    angles = product.astype(jnp.float32) * (2.0 * math.pi / length)
    return (jnp.cos(angles).astype(jnp.bfloat16), jnp.sin(angles).astype(jnp.bfloat16))


def signed_waves(series, length):
    signed = jnp.where(series < length // 2, series, series - length)
    signed = jnp.where(series == length // 2, 0, signed)
    return signed.astype(jnp.float32) * (2.0 * math.pi / length)


def wave_numbers(length):
    return signed_waves(jnp.arange(length, dtype=jnp.int32), length)


def cubic_table(levels):
    fraction = (jnp.arange(levels, dtype=jnp.float32) + 0.5) / levels
    node_left = -fraction * (fraction - 1.0) * (fraction - 2.0) / 6.0
    node_zero = (fraction + 1.0) * (fraction - 1.0) * (fraction - 2.0) / 2.0
    node_one = -(fraction + 1.0) * fraction * (fraction - 2.0) / 2.0
    node_two = (fraction + 1.0) * fraction * (fraction - 1.0) / 6.0
    return jnp.stack([node_left, node_zero, node_one, node_two], axis=1)


def pick_weights(weight_level, weight_table):
    onehot = (
        weight_level[:, None] == jnp.arange(weight_table.shape[0], dtype=jnp.int32)[None, :]
    ).astype(jnp.float32)
    return jnp.dot(onehot, weight_table, precision=lax.Precision.HIGHEST)


def local(template, reference_image, velocity, dep_owner, dep_offset, dep_weight):
    peer_count = lax.axis_size("pencil")
    row_count, plane_count, y_count = template.shape
    full_rows = row_count * peer_count
    z_groups = plane_count // ZB
    y_groups = y_count // SEG
    per_row = z_groups * y_groups
    block_count = row_count * per_row
    cell_count = plane_count * y_count
    weight_table = cubic_table(Q)
    my_index = lax.axis_index("pencil")
    shaped = template.reshape(row_count, z_groups, ZB, y_groups, SEG)
    blocks = shaped.transpose(0, 1, 3, 2, 4).reshape(block_count, ZB * SEG)
    for section_index in range(2):
        pieces = []
        for distance in (2, 1, 0, -1, -2):
            if distance == 0:
                pieces.append(blocks)
            else:
                pieces.append(shifted(blocks, "pencil", distance))
        window = jnp.concatenate(pieces, axis=0)
        relative = (dep_owner[section_index] - my_index + peer_count) % peer_count
        move = jnp.where(relative >= peer_count - 2, relative - peer_count, relative)
        offset = dep_offset[section_index]
        start_row = offset // per_row
        place = offset % per_row
        tap_row = (
            (move[:, None] + 2) * row_count
            + start_row[:, None]
            + jnp.arange(4, dtype=jnp.int32)[None, :]
        )
        taps = window[tap_row * per_row + place[:, None]].astype(jnp.float32)
        weights = pick_weights(dep_weight[section_index], weight_table)
        blocks = jnp.sum(weights[:, :, None] * taps, axis=1).astype(jnp.bfloat16)
    shaped = blocks.reshape(row_count, z_groups, y_groups, ZB, SEG)
    warped = shaped.transpose(0, 1, 3, 2, 4).reshape(row_count, plane_count, y_count)
    warped_f = warped.astype(jnp.float32)
    residual = reference_image.astype(jnp.float32) - warped_f
    cos_y, sin_y = dft_tables(y_count)
    cos_x, sin_x = dft_tables(full_rows)
    kvec_y = wave_numbers(y_count)
    kvec_x = wave_numbers(full_rows)
    forward_y = jnp.concatenate([cos_y, -sin_y], axis=1)
    inverse_y = jnp.concatenate([cos_y, -sin_y], axis=0)
    forward_x = jnp.concatenate([cos_x, -sin_x], axis=0)
    inverse_x = jnp.concatenate([cos_x, -sin_x], axis=1)
    spec_y = jnp.dot(warped.reshape(-1, y_count), forward_y, preferred_element_type=jnp.float32)
    spec_y = spec_y.astype(jnp.bfloat16).astype(jnp.float32)
    coef_y = jnp.concatenate(
        [-kvec_y * spec_y[:, y_count:], kvec_y * spec_y[:, :y_count]], axis=1
    ).astype(jnp.bfloat16)
    slope_y = (jnp.dot(coef_y, inverse_y, preferred_element_type=jnp.float32) / y_count).reshape(
        row_count, plane_count, y_count
    )
    flat_warp = warped.reshape(1, row_count, cell_count)
    spec_x = jnp.einsum(
        "kx,ixm->ikm",
        forward_x,
        lax.all_to_all(flat_warp, "pencil", split_axis=2, concat_axis=1, tiled=True),
        preferred_element_type=jnp.float32,
    )
    coef_x = jnp.concatenate(
        [
            -kvec_x[None, :, None] * spec_x[:, full_rows:],
            kvec_x[None, :, None] * spec_x[:, :full_rows],
        ],
        axis=1,
    ).astype(jnp.bfloat16)
    slope = (
        jnp.einsum("xk,ikm->ixm", inverse_x, coef_x, preferred_element_type=jnp.float32) / full_rows
    ).astype(jnp.bfloat16)
    slope_x = lax.all_to_all(slope, "pencil", split_axis=1, concat_axis=2, tiled=True)
    slope_x = slope_x.reshape(row_count, plane_count, y_count)
    slope_z = (jnp.roll(warped_f, -1, axis=1) - jnp.roll(warped_f, 1, axis=1)) * 0.5
    force = (jnp.stack([slope_x.astype(jnp.float32), slope_y, slope_z]) * residual[None]).astype(
        jnp.bfloat16
    )
    force_lines = force.reshape(-1, y_count)
    spec_real = jnp.dot(force_lines, cos_y, preferred_element_type=jnp.float32).astype(jnp.bfloat16)
    spec_imag = jnp.dot(force_lines, -sin_y, preferred_element_type=jnp.float32).astype(
        jnp.bfloat16
    )
    spec_f = jnp.stack(
        [spec_real.reshape(3, row_count, cell_count), spec_imag.reshape(3, row_count, cell_count)],
        axis=1,
    )
    planes = lax.all_to_all(spec_f, "pencil", split_axis=3, concat_axis=2, tiled=True)
    local_cols = planes.shape[3]
    column_ids = my_index * local_cols + jnp.arange(local_cols, dtype=jnp.int32)
    kvec_local = signed_waves(column_ids % y_count, y_count)
    spectral_gain = force_gain / (
        full_rows
        * y_count
        * (
            1.0
            + h1_weight
            * (kvec_x[:, None] * kvec_x[:, None] + kvec_local[None, :] * kvec_local[None, :])
        )
    )
    cos_part = jnp.einsum("kx,chxm->chkm", cos_x, planes, preferred_element_type=jnp.float32)
    sin_part = jnp.einsum("kx,chxm->chkm", sin_x, planes, preferred_element_type=jnp.float32)
    real_f = cos_part[:, 0] + sin_part[:, 1]
    imag_f = cos_part[:, 1] - sin_part[:, 0]
    scale_grid = spectral_gain[None]
    scaled = jnp.stack([real_f * scale_grid, imag_f * scale_grid], axis=1).astype(jnp.bfloat16)
    cos_back = jnp.einsum("xk,chkm->chxm", cos_x, scaled, preferred_element_type=jnp.float32)
    sin_back = jnp.einsum("xk,chkm->chxm", sin_x, scaled, preferred_element_type=jnp.float32)
    real_b = cos_back[:, 0] - sin_back[:, 1]
    imag_b = cos_back[:, 1] + sin_back[:, 0]
    mixed = jnp.stack([real_b, imag_b], axis=1).astype(jnp.bfloat16)
    smoothed = lax.all_to_all(mixed, "pencil", split_axis=2, concat_axis=3, tiled=True)
    spatial = jnp.dot(
        smoothed[:, 0].reshape(-1, y_count), cos_y, preferred_element_type=jnp.float32
    )
    spatial = spatial - jnp.dot(
        smoothed[:, 1].reshape(-1, y_count), sin_y, preferred_element_type=jnp.float32
    )
    gradient = velocity + spatial.reshape(3, row_count, plane_count, y_count)
    return (warped, gradient)


def solution(mesh):
    in_specs = (
        P("pencil", "start", None),
        P("pencil", "start", None),
        P("start", "pencil", None, None),
        P("start", "pencil"),
        P("start", "pencil"),
        P("start", "pencil"),
    )
    out_specs = (P("pencil", "start", None), P("start", "pencil", None, None))
    return jax.shard_map(local, mesh=mesh, in_specs=in_specs, out_specs=out_specs, check_vma=False)
```

profile of v0, /device:TPU:2, one launch (start us, length us, event | category | flops | bytes accessed | tf_op | source)
XLA Modules:
  0.0 645.6 jit_solution(7379281555663057057)
XLA Ops:
  45.5 12.9 %copy.100 = bf16[1,4,16384]{1,0,2:T(2,128)(2,1)} copy(bf16[1,4,16384]{2,1,0:T(4,128)(2,1)S(1)} %reshape_reshape.6) | data formatting | bytes 262144 | tf_op jit(solution)/shard_map/reshape;reshape | solution.py:106
  58.9 90.7 %reduce = bf16[16384,4]{1,0:T(8,128)(2,1)} reduce(bf16[16384,1,4]{2,1,0:T(2,128)(2,1)} %bitcast.108, bf16[]{:T(256)} %broadcast.922), dimensions={1}, to_apply=%bitcast.90.reduce_sub_computation | reduce | bytes 262146
  149.6 9.3 %reshape.616 = bf16[128,2,256]{2,1,0:T(2,128)(2,1)} reshape(bf16[16384,4]{1,0:T(8,128)(2,1)} %reduce) | data formatting | bytes 262144
  158.9 19.8 %all-to-all-start = ((bf16[128,2,256]{2,1,0:T(2,128)(2,1)}), bf16[128,2,256]{2,1,0:T(2,128)(2,1)S(1)}, u32[]{:S(2)}, u32[]{:S(2)}) async-start(bf16[128,2,256]{2,1,0:T(2,128)(2,1)} %reshape.616), calls=%async_computation | async-start | bytes 262144 | tf_op jit(solution)/shard_map/all_to_all | solution.py:110
  179.5 11.0 %all-to-all-done = bf16[128,2,256]{2,1,0:T(2,128)(2,1)S(1)} async-done(((bf16[128,2,256]{2,1,0:T(2,128)(2,1)}), bf16[128,2,256]{2,1,0:T(2,128)(2,1)S(1)}, u32[]{:S(2)}, u32[]{:S(2)}) %all-to-all-start) | async-done | bytes 131104 | tf_op jit(solution)/shard_map/all_to_all | solution.py:110
  190.4 17.1 %reshape.617 = bf16[16384,1,4]{2,1,0:T(2,128)(2,1)} reshape(bf16[128,2,256]{2,1,0:T(2,128)(2,1)S(1)} %all-to-all-done) | data formatting | bytes 262144
  207.5 15.4 %copy.101 = bf16[1,4,16384]{2,1,0:T(4,128)(2,1)S(1)} copy(bf16[1,4,16384]{1,0,2:T(2,128)(2,1)} %bitcast.109) | data formatting | bytes 262144 | tf_op jit(solution)/shard_map/all_to_all | solution.py:110
  226.4 6.6 %all-to-all-start.1 = ((bf16[128,2,256]{2,1,0:T(2,128)(2,1)}), bf16[128,2,256]{2,1,0:T(2,128)(2,1)S(1)}, u32[]{:S(2)}, u32[]{:S(2)}) async-start(bf16[128,2,256]{2,1,0:T(2,128)(2,1)} %reshape.618), calls=%async_computation.1 | async-start | bytes 262144 | tf_op jit(solution)/shard_map/all_to_all | solution.py:123
  233.1 11.8 %all-to-all-done.1 = bf16[128,2,256]{2,1,0:T(2,128)(2,1)S(1)} async-done(((bf16[128,2,256]{2,1,0:T(2,128)(2,1)}), bf16[128,2,256]{2,1,0:T(2,128)(2,1)S(1)}, u32[]{:S(2)}, u32[]{:S(2)}) %all-to-all-start.1) | async-done | bytes 131104 | tf_op jit(solution)/shard_map/all_to_all | solution.py:123
  245.3 4.8 convolution_convert_fusion.1
  250.1 4.9 convolution_convert_fusion
  255.3 39.4 %copy.107 = bf16[3,1,4,16384]{2,1,0,3:T(2,128)(2,1)} copy(bf16[3,1,4,16384]{3,2,0,1:T(4,128)(2,1)S(1)} %stack_reshape.10) | data formatting | bytes 786432 | tf_op jit(solution)/shard_map/stack;reshape | solution.py:134
  294.9 39.6 %copy.108 = bf16[3,1,4,16384]{2,1,0,3:T(2,128)(2,1)} copy(bf16[3,1,4,16384]{3,2,0,1:T(4,128)(2,1)S(1)} %stack_reshape.11) | data formatting | bytes 786432 | tf_op jit(solution)/shard_map/stack;reshape | solution.py:134
  334.5 70.4 %fusion.102 = bf16[16384,3,2,4]{3,2,1,0:T(2,128)(2,1)} fusion(bf16[3,1,4,16384]{2,1,0,3:T(2,128)(2,1)} %copy.108, bf16[3,1,4,16384]{2,1,0,3:T(2,128)(2,1)} %copy.107), kind=kLoop, calls=%fused_computation.201 | loop fusion | flops 1572864 | bytes 1572864
  404.9 61.9 %reshape.620 = bf16[128,2,1536]{2,1,0:T(2,128)(2,1)} reshape(bf16[16384,3,2,4]{3,2,1,0:T(2,128)(2,1)} %fusion.102) | data formatting | bytes 1572864
  466.8 7.0 %all-to-all-start.2 = ((bf16[128,2,1536]{2,1,0:T(2,128)(2,1)}), bf16[128,2,1536]{2,1,0:T(2,128)(2,1)S(1)}, u32[]{:S(2)}, u32[]{:S(2)}) async-start(bf16[128,2,1536]{2,1,0:T(2,128)(2,1)} %reshape.620), calls=%async_computation.2 | async-start | bytes 1572864 | tf_op jit(solution)/shard_map/all_to_all | solution.py:138
  474.0 20.2 %all-to-all-done.2 = bf16[128,2,1536]{2,1,0:T(2,128)(2,1)S(1)} async-done(((bf16[128,2,1536]{2,1,0:T(2,128)(2,1)}), bf16[128,2,1536]{2,1,0:T(2,128)(2,1)S(1)}, u32[]{:S(2)}, u32[]{:S(2)}) %all-to-all-start.2) | async-done | bytes 786464 | tf_op jit(solution)/shard_map/all_to_all | solution.py:138
  494.2 55.1 %reshape.621 = bf16[16384,3,2,4]{3,2,1,0:T(2,128)(2,1)} reshape(bf16[128,2,1536]{2,1,0:T(2,128)(2,1)S(1)} %all-to-all-done.2) | data formatting | bytes 1572864
  549.3 35.1 %copy.121 = bf16[3,2,4,128,128]{4,3,2,1,0:T(8,128)(2,1)S(1)} copy(bf16[3,2,4,128,128]{2,1,0,4,3:T(2,128)(2,1)} %bitcast.107) | data formatting | bytes 1572864 | tf_op jit(solution)/shard_map/all_to_all | solution.py:138
  585.0 5.5 convolution_bitcast_fusion.2
  590.5 5.9 convolution_bitcast_fusion.3
  607.1 27.0 %all_to_all.60 = bf16[3,2,512,128]{3,1,0,2:T(2,128)(2,1)S(1)} all-to-all(bf16[3,2,512,128]{3,1,0,2:T(2,128)(2,1)S(1)} %copy.113), channel_id=1, replica_groups=mesh['start'=2,'pencil'=128] {'pencil'}, dimensions={2} | all-to-all | bytes 1572864 | tf_op jit(solution)/shard_map/all_to_all | solution.py:162
  634.8 4.6 fusion.21
  639.7 4.7 convolution_subtract_fusion
  (103 shorter events, 63.5 us)
Async XLA Ops:
  1.7 14.8 %collective-permute-start = (bf16[256,256]{1,0:T(8,128)(2,1)S(1)}, bf16[256,256]{1,0:T(8,128)(2,1)S(1)}, u32[]{:S(2)}, u32[]{:S(2)}) collective-permute-start(bf16[256,256]{1,0:T(8,128)(2,1)S(1)} %bitcast.127), channel_id=1, source_target_pairs={{0,2},{1,3},{2,4},{3,5},{4,6},{5,7},{6,8},{7,9},{8,10},{9,11},{10,... | collective-permute-start | bytes 393224 | tf_op jit(solution)/shard_map/ppermute | solution.py:16
  5.0 11.5 %collective-permute-start.1 = (bf16[256,256]{1,0:T(8,128)(2,1)S(1)}, bf16[256,256]{1,0:T(8,128)(2,1)S(1)}, u32[]{:S(2)}, u32[]{:S(2)}) collective-permute-start(bf16[256,256]{1,0:T(8,128)(2,1)S(1)} %bitcast.128), channel_id=1, source_target_pairs={{0,1},{1,2},{2,3},{3,4},{4,5},{5,6},{6,7},{7,8},{8,9},{9,10},{10,1... | collective-permute-start | bytes 393224 | tf_op jit(solution)/shard_map/ppermute | solution.py:16
  5.7 10.9 %collective-permute-start.2 = (bf16[256,256]{1,0:T(8,128)(2,1)S(1)}, bf16[256,256]{1,0:T(8,128)(2,1)S(1)}, u32[]{:S(2)}, u32[]{:S(2)}) collective-permute-start(bf16[256,256]{1,0:T(8,128)(2,1)S(1)} %bitcast.129), channel_id=1, source_target_pairs={{0,127},{1,0},{2,1},{3,2},{4,3},{5,4},{6,5},{7,6},{8,7},{9,8},{10,... | collective-permute-start | bytes 393224 | tf_op jit(solution)/shard_map/ppermute | solution.py:16
  9.1 7.5 %collective-permute-start.3 = (bf16[256,256]{1,0:T(8,128)(2,1)S(1)}, bf16[256,256]{1,0:T(8,128)(2,1)S(1)}, u32[]{:S(2)}, u32[]{:S(2)}) collective-permute-start(bf16[256,256]{1,0:T(8,128)(2,1)S(1)} %bitcast.130), channel_id=1, source_target_pairs={{0,126},{1,127},{2,0},{3,1},{4,2},{5,3},{6,4},{7,5},{8,6},{9,7},{1... | collective-permute-start | bytes 393224 | tf_op jit(solution)/shard_map/ppermute | solution.py:16
  21.6 13.5 %collective-permute-start.4 = (bf16[256,256]{1,0:T(8,128)(2,1)S(1)}, bf16[256,256]{1,0:T(8,128)(2,1)S(1)}, u32[]{:S(2)}, u32[]{:S(2)}) collective-permute-start(bf16[256,256]{1,0:T(8,128)(2,1)S(1)} %multiply_reduce_fusion.1), channel_id=1, source_target_pairs={{0,2},{1,3},{2,4},{3,5},{4,6},{5,7},{6,8},{7,9},{8,10},{9,11},{10,... | collective-permute-start | bytes 393224 | tf_op jit(solution)/shard_map/ppermute | solution.py:16
  29.2 7.7 %collective-permute-start.5 = (bf16[256,256]{1,0:T(8,128)(2,1)S(1)}, bf16[256,256]{1,0:T(8,128)(2,1)S(1)}, u32[]{:S(2)}, u32[]{:S(2)}) collective-permute-start(bf16[256,256]{1,0:T(8,128)(2,1)S(1)} %multiply_reduce_fusion.1), channel_id=1, source_target_pairs={{0,1},{1,2},{2,3},{3,4},{4,5},{5,6},{6,7},{7,8},{8,9},{9,10},{10,1... | collective-permute-start | bytes 393224 | tf_op jit(solution)/shard_map/ppermute | solution.py:16
  29.3 7.6 %collective-permute-start.6 = (bf16[256,256]{1,0:T(8,128)(2,1)S(1)}, bf16[256,256]{1,0:T(8,128)(2,1)S(1)}, u32[]{:S(2)}, u32[]{:S(2)}) collective-permute-start(bf16[256,256]{1,0:T(8,128)(2,1)S(1)} %multiply_reduce_fusion.1), channel_id=1, source_target_pairs={{0,127},{1,0},{2,1},{3,2},{4,3},{5,4},{6,5},{7,6},{8,7},{9,8},{10,... | collective-permute-start | bytes 393224 | tf_op jit(solution)/shard_map/ppermute | solution.py:16
  33.4 6.9 %collective-permute-start.7 = (bf16[256,256]{1,0:T(8,128)(2,1)S(1)}, bf16[256,256]{1,0:T(8,128)(2,1)S(1)}, u32[]{:S(2)}, u32[]{:S(2)}) collective-permute-start(bf16[256,256]{1,0:T(8,128)(2,1)S(1)} %multiply_reduce_fusion.1), channel_id=1, source_target_pairs={{0,126},{1,127},{2,0},{3,1},{4,2},{5,3},{6,4},{7,5},{8,6},{9,7},{1... | collective-permute-start | bytes 393224 | tf_op jit(solution)/shard_map/ppermute | solution.py:16
  45.5 187.6 %copy-start = (bf16[4,32,512]{2,1,0:T(8,128)(2,1)}, bf16[4,32,512]{2,1,0:T(8,128)(2,1)S(1)}, u32[]{:S(2)}) copy-start(bf16[4,32,512]{2,1,0:T(8,128)(2,1)S(1)} %reshape.589) | copy-start | bytes 393220
  158.9 31.5 %all-to-all-start = ((bf16[128,2,256]{2,1,0:T(2,128)(2,1)}), bf16[128,2,256]{2,1,0:T(2,128)(2,1)S(1)}, u32[]{:S(2)}, u32[]{:S(2)}) async-start(bf16[128,2,256]{2,1,0:T(2,128)(2,1)} %reshape.616), calls=%async_computation | async-start | bytes 262144 | tf_op jit(solution)/shard_map/all_to_all | solution.py:110
  223.6 9.4 %copy-start.2 = (bf16[4,32,512]{2,1,0:T(8,128)(2,1)S(1)}, bf16[4,32,512]{2,1,0:T(8,128)(2,1)}, u32[]{:S(2)}) copy-start(bf16[4,32,512]{2,1,0:T(8,128)(2,1)} %param.7) | copy-start | bytes 393220
  226.4 18.5 %all-to-all-start.1 = ((bf16[128,2,256]{2,1,0:T(2,128)(2,1)}), bf16[128,2,256]{2,1,0:T(2,128)(2,1)S(1)}, u32[]{:S(2)}, u32[]{:S(2)}) async-start(bf16[128,2,256]{2,1,0:T(2,128)(2,1)} %reshape.618), calls=%async_computation.1 | async-start | bytes 262144 | tf_op jit(solution)/shard_map/all_to_all | solution.py:123
  466.8 27.4 %all-to-all-start.2 = ((bf16[128,2,1536]{2,1,0:T(2,128)(2,1)}), bf16[128,2,1536]{2,1,0:T(2,128)(2,1)S(1)}, u32[]{:S(2)}, u32[]{:S(2)}) async-start(bf16[128,2,1536]{2,1,0:T(2,128)(2,1)} %reshape.620), calls=%async_computation.2 | async-start | bytes 1572864 | tf_op jit(solution)/shard_map/all_to_all | solution.py:138
  639.7 4.7 copy-start.1
where the time goes:
time: 654 us; the launch traced here: 646 us
  local copies, waits for them, and re-layouts  302 us (46%)
  other arithmetic  175 us (27%)
  starting transfers between devices  50.2 us (8%)
  waiting for transfers between devices  48.2 us (7%)
  matrix products  41.1 us (6%)
  blocking collectives  27 us (4%)
    unnamed x3, other arithmetic  162 us
    unnamed x23, local copies, waits for them, and re-layouts  145 us
    another operation x4, local copies, waits for them, and re-layouts, local(): jnp.stack([spec_real.reshape(3, row_count, cell_count), spec_imag.reshape...  79.5 us
    all_to_all x2, local copies, waits for them, and re-layouts, local(): lax.all_to_all(spec_f, 'pencil', split_axis=3, concat_axis=2, tiled=True)  35.7 us
    all_to_all x1, blocking collectives, local(): lax.all_to_all(mixed, 'pencil', split_axis=2, concat_axis=3, tiled=True)  27 us
    all_to_all x1, waiting for transfers between devices, local(): lax.all_to_all(spec_f, 'pencil', split_axis=3, concat_axis=2, tiled=True)  20.2 us
    all_to_all x1, starting transfers between devices, local(): lax.all_to_all(flat_warp, 'pencil', split_axis=2, concat_axis=1, tiled=True)  19.8 us
    ppermute x8, starting transfers between devices, shifted(): lax.ppermute(x, axis, [(i, (i + by) % length) for i in range(length)])  16.9 us
  transfers between devices with their start and end apart: 11, of which 5 were waited for; matrix products, arithmetic and copies ran while one was open for 2% of the time, Pallas kernels for 0%

commit v1 on v0

--- a/solution.py
+++ b/solution.py
@@ -135,7 +135,12 @@
         [spec_real.reshape(3, row_count, cell_count), spec_imag.reshape(3, row_count, cell_count)],
         axis=1,
     )
-    planes = lax.all_to_all(spec_f, "pencil", split_axis=3, concat_axis=2, tiled=True)
+    planes = jnp.concatenate(
+        lax.all_to_all(
+            jnp.stack(jnp.split(spec_f, lax.axis_size("pencil"), axis=3)), "pencil", 0, 0
+        ),
+        axis=2,
+    )
     local_cols = planes.shape[3]
     column_ids = my_index * local_cols + jnp.arange(local_cols, dtype=jnp.int32)
     kvec_local = signed_waves(column_ids % y_count, y_count)

time: 654 us -> 440 us (0.67)
  local copies, waits for them, and re-layouts: 302 us -> 70.9 us
  starting transfers between devices: 50.2 us -> 61.3 us
  other arithmetic: 175 us -> 182 us
    unnamed x23 -> x21, local copies, waits for them, and re-layouts: 145 us -> 27.9 us
    another operation x4 -> x2, local copies, waits for them, and re-layouts: 79.5 us -> 0.57 us  [local(): jnp.stack([spec_real.reshape(3, row_count, cell_count), spec_imag.reshape...]
    all_to_all x2 -> x0, local copies, waits for them, and re-layouts: 35.7 us -> none  [local(): lax.all_to_all(spec_f, 'pencil', split_axis=3, concat_axis=2, tiled=True)]
    all_to_all x1, starting transfers between devices: 19.8 us -> 31.4 us  [local(): lax.all_to_all(flat_warp, 'pencil', split_axis=2, concat_axis=1, tiled=True)]
    unnamed x3 -> x129, other arithmetic: 162 us -> 168 us
  transfers between devices with their start and end apart: 11 -> 11, of which waited for: 5 -> 5; matrix products, arithmetic and copies ran while one was open for 2% -> 3% of each run, Pallas kernels for 0% -> 0%
where the time goes in v1:
time: 440 us; the launch traced here: 432 us
  other arithmetic  182 us (41%)
  local copies, waits for them, and re-layouts  70.9 us (16%)
  starting transfers between devices  61.3 us (14%)
  waiting for transfers between devices  48.3 us (11%)
  matrix products  40.9 us (9%)
  blocking collectives  27.1 us (6%)
    unnamed x129, other arithmetic  168 us
    all_to_all x1, starting transfers between devices, local(): lax.all_to_all(flat_warp, 'pencil', split_axis=2, concat_axis=1, tiled=True)  31.4 us
    unnamed x21, local copies, waits for them, and re-layouts  27.9 us
    all_to_all x1, blocking collectives, local(): lax.all_to_all(mixed, 'pencil', split_axis=2, concat_axis=3, tiled=True)  27.1 us
    all_to_all x1, waiting for transfers between devices, local(): lax.all_to_all(jnp.stack(jnp.split(spec_f, lax.axis_size('pencil'), axis=...  20.3 us
    ppermute x8, starting transfers between devices, shifted(): lax.ppermute(x, axis, [(i, (i + by) % length) for i in range(length)])  16.7 us
    all_to_all x2, local copies, waits for them, and re-layouts, local(): lax.all_to_all(flat_warp, 'pencil', split_axis=2, concat_axis=1, tiled=True)  15.5 us
    another operation x2, local copies, waits for them, and re-layouts, local(): flat_warp = warped.reshape(1, row_count, cell_count)  13 us
  transfers between devices with their start and end apart: 11, of which 5 were waited for; matrix products, arithmetic and copies ran while one was open for 3% of the time, Pallas kernels for 0%

profile of v1, /device:TPU:2, one launch (start us, length us, event | category | flops | bytes accessed | tf_op | source)
XLA Modules:
  0.0 431.9 jit_solution(3721829388552712221)
XLA Ops:
  16.6 3.9 gather_fusion
  25.2 4.0 fusion.20
  29.3 4.1 collective-permute-start.6
  40.1 3.9 gather_fusion.1
  45.3 12.9 %copy.313 = bf16[1,4,16384]{1,0,2:T(2,128)(2,1)} copy(bf16[1,4,16384]{2,1,0:T(4,128)(2,1)S(1)} %reshape_reshape.6) | data formatting | bytes 262144 | tf_op jit(solution)/shard_map/reshape;reshape | solution.py:106
  58.7 90.7 %reduce = bf16[16384,4]{1,0:T(8,128)(2,1)} reduce(bf16[16384,1,4]{2,1,0:T(2,128)(2,1)} %bitcast.619, bf16[]{:T(256)} %broadcast.922), dimensions={1}, to_apply=%bitcast.349.reduce_sub_computation | reduce | bytes 262146
  149.4 9.3 %reshape.624 = bf16[128,2,256]{2,1,0:T(2,128)(2,1)} reshape(bf16[16384,4]{1,0:T(8,128)(2,1)} %reduce) | data formatting | bytes 262144
  158.7 31.4 %all-to-all-start = ((bf16[128,2,256]{2,1,0:T(2,128)(2,1)}), bf16[128,2,256]{2,1,0:T(2,128)(2,1)S(1)}, u32[]{:S(2)}, u32[]{:S(2)}) async-start(bf16[128,2,256]{2,1,0:T(2,128)(2,1)} %reshape.624), calls=%async_computation | async-start | bytes 262144 | tf_op jit(solution)/shard_map/all_to_all | solution.py:110
  190.8 11.0 %all-to-all-done = bf16[128,2,256]{2,1,0:T(2,128)(2,1)S(1)} async-done(((bf16[128,2,256]{2,1,0:T(2,128)(2,1)}), bf16[128,2,256]{2,1,0:T(2,128)(2,1)S(1)}, u32[]{:S(2)}, u32[]{:S(2)}) %all-to-all-start) | async-done | bytes 131104 | tf_op jit(solution)/shard_map/all_to_all | solution.py:110
  201.8 17.1 %reshape.625 = bf16[16384,1,4]{2,1,0:T(2,128)(2,1)} reshape(bf16[128,2,256]{2,1,0:T(2,128)(2,1)S(1)} %all-to-all-done) | data formatting | bytes 262144
  218.9 15.4 %copy.314 = bf16[1,4,16384]{2,1,0:T(4,128)(2,1)S(1)} copy(bf16[1,4,16384]{1,0,2:T(2,128)(2,1)} %bitcast.620) | data formatting | bytes 262144 | tf_op jit(solution)/shard_map/all_to_all | solution.py:110
  237.7 6.6 %all-to-all-start.1 = ((bf16[128,2,256]{2,1,0:T(2,128)(2,1)}), bf16[128,2,256]{2,1,0:T(2,128)(2,1)S(1)}, u32[]{:S(2)}, u32[]{:S(2)}) async-start(bf16[128,2,256]{2,1,0:T(2,128)(2,1)} %reshape.626), calls=%async_computation.1 | async-start | bytes 262144 | tf_op jit(solution)/shard_map/all_to_all | solution.py:123
  244.5 11.8 %all-to-all-done.1 = bf16[128,2,256]{2,1,0:T(2,128)(2,1)S(1)} async-done(((bf16[128,2,256]{2,1,0:T(2,128)(2,1)}), bf16[128,2,256]{2,1,0:T(2,128)(2,1)S(1)}, u32[]{:S(2)}, u32[]{:S(2)}) %all-to-all-start.1) | async-done | bytes 131104 | tf_op jit(solution)/shard_map/all_to_all | solution.py:123
  256.6 4.8 %convolution_convert_fusion.1 = bf16[384,512]{1,0:T(8,128)(2,1)S(1)} fusion(bf16[384,512]{1,0:T(8,128)(2,1)S(1)} %bitcast.635), kind=kOutput, calls=%fused_computation.265 | convolution fusion | flops 205455360 | bytes 786432 | tf_op jit(solution)/shard_map/dot_general | solution.py:130
  261.5 4.9 %convolution_convert_fusion = bf16[384,512]{1,0:T(8,128)(2,1)S(1)} fusion(bf16[384,512]{1,0:T(8,128)(2,1)S(1)} %bitcast.636), kind=kOutput, calls=%fused_computation.264 | convolution fusion | flops 206241792 | bytes 786432 | tf_op jit(solution)/shard_map/dot_general | solution.py:131
  343.7 6.6 %all-to-all-start.2 = ((bf16[128,3,2,4,128]{4,3,2,1,0:T(4,128)(2,1)}), bf16[128,3,2,4,128]{4,3,2,1,0:T(4,128)(2,1)S(1)}, u32[]{:S(2)}, u32[]{:S(2)}) async-start(bf16[128,3,2,4,128]{4,3,2,1,0:T(4,128)(2,1)} %constant_dynamic-update-slice_fusion.10), calls=%async_computation.2 | async-start | bytes 1572864 | tf_op jit(solution)/shard_map/all_to_all | solution.py:139
  350.5 20.3 %all-to-all-done.2 = bf16[128,3,2,4,128]{4,3,2,1,0:T(4,128)(2,1)S(1)} async-done(((bf16[128,3,2,4,128]{4,3,2,1,0:T(4,128)(2,1)}), bf16[128,3,2,4,128]{4,3,2,1,0:T(4,128)(2,1)S(1)}, u32[]{:S(2)}, u32[]{:S(2)}) %all-to-all-start.2) | async-done | bytes 786464 | tf_op jit(solution)/shard_map/all_to_all | solution.py:139
  371.1 5.6 %convolution_bitcast_fusion.2 = f32[3,2,512,128]{2,3,1,0:T(8,128)S(1)} fusion(bf16[3,2,512,128]{3,2,1,0:T(8,128)(2,1)S(1)} %bitcast.628), kind=kOutput, calls=%fused_computation.261 | convolution fusion | flops 406585344 | bytes 2359296 | tf_op jit(solution)/shard_map/kx,chxm->chkm/dot_general | solution.py:157
  376.6 5.7 %convolution_bitcast_fusion.3 = f32[3,2,512,128]{2,3,1,0:T(8,128)S(1)} fusion(bf16[3,2,512,128]{3,2,1,0:T(8,128)(2,1)S(1)} %bitcast.629), kind=kOutput, calls=%fused_computation.262 | convolution fusion | flops 406585344 | bytes 2359296 | tf_op jit(solution)/shard_map/kx,chxm->chkm/dot_general | solution.py:156
  382.8 4.3 convolution_bitcast_fusion.1
  387.1 4.3 convolution_bitcast_fusion
  393.0 27.1 %all_to_all.47 = bf16[3,2,512,128]{3,1,0,2:T(2,128)(2,1)S(1)} all-to-all(bf16[3,2,512,128]{3,1,0,2:T(2,128)(2,1)S(1)} %copy.325), channel_id=1, replica_groups=mesh['start'=2,'pencil'=128] {'pencil'}, dimensions={2} | all-to-all | bytes 1572864 | tf_op jit(solution)/shard_map/all_to_all | solution.py:167
  420.8 4.6 %fusion.21 = f32[384,512]{1,0:T(8,128)S(1)} fusion(bf16[384,512]{1,0:T(8,128)(2,1)S(1)} %reshape_squeeze.6), kind=kOutput, calls=%fused_computation.304 | convolution fusion | flops 205258752 | bytes 1179648 | tf_op jit(solution)/shard_map/dot_general | solution.py:168
  425.7 4.7 %convolution_subtract_fusion = f32[384,512]{1,0:T(8,128)S(1)} fusion(f32[384,512]{1,0:T(8,128)S(1)} %fusion.21, bf16[384,512]{1,0:T(8,128)(2,1)S(1)} %reshape_squeeze.7), kind=kOutput, calls=%fused_computation.263 | convolution fusion | flops 205455360 | bytes 1966080 | tf_op jit(solution)/shard_map/dot_general | solution.py:171
  (225 shorter events, 115.1 us)
Async XLA Ops:
  1.7 14.8 %collective-permute-start = (bf16[256,256]{1,0:T(8,128)(2,1)S(1)}, bf16[256,256]{1,0:T(8,128)(2,1)S(1)}, u32[]{:S(2)}, u32[]{:S(2)}) collective-permute-start(bf16[256,256]{1,0:T(8,128)(2,1)S(1)} %bitcast.638), channel_id=1, source_target_pairs={{0,2},{1,3},{2,4},{3,5},{4,6},{5,7},{6,8},{7,9},{8,10},{9,11},{10,... | collective-permute-start | bytes 393224 | tf_op jit(solution)/shard_map/ppermute | solution.py:16
  5.0 11.5 %collective-permute-start.1 = (bf16[256,256]{1,0:T(8,128)(2,1)S(1)}, bf16[256,256]{1,0:T(8,128)(2,1)S(1)}, u32[]{:S(2)}, u32[]{:S(2)}) collective-permute-start(bf16[256,256]{1,0:T(8,128)(2,1)S(1)} %bitcast.639), channel_id=1, source_target_pairs={{0,1},{1,2},{2,3},{3,4},{4,5},{5,6},{6,7},{7,8},{8,9},{9,10},{10,1... | collective-permute-start | bytes 393224 | tf_op jit(solution)/shard_map/ppermute | solution.py:16
  5.7 10.9 %collective-permute-start.2 = (bf16[256,256]{1,0:T(8,128)(2,1)S(1)}, bf16[256,256]{1,0:T(8,128)(2,1)S(1)}, u32[]{:S(2)}, u32[]{:S(2)}) collective-permute-start(bf16[256,256]{1,0:T(8,128)(2,1)S(1)} %bitcast.640), channel_id=1, source_target_pairs={{0,127},{1,0},{2,1},{3,2},{4,3},{5,4},{6,5},{7,6},{8,7},{9,8},{10,... | collective-permute-start | bytes 393224 | tf_op jit(solution)/shard_map/ppermute | solution.py:16
  9.1 7.5 %collective-permute-start.3 = (bf16[256,256]{1,0:T(8,128)(2,1)S(1)}, bf16[256,256]{1,0:T(8,128)(2,1)S(1)}, u32[]{:S(2)}, u32[]{:S(2)}) collective-permute-start(bf16[256,256]{1,0:T(8,128)(2,1)S(1)} %bitcast.641), channel_id=1, source_target_pairs={{0,126},{1,127},{2,0},{3,1},{4,2},{5,3},{6,4},{7,5},{8,6},{9,7},{1... | collective-permute-start | bytes 393224 | tf_op jit(solution)/shard_map/ppermute | solution.py:16
  21.6 13.3 %collective-permute-start.4 = (bf16[256,256]{1,0:T(8,128)(2,1)S(1)}, bf16[256,256]{1,0:T(8,128)(2,1)S(1)}, u32[]{:S(2)}, u32[]{:S(2)}) collective-permute-start(bf16[256,256]{1,0:T(8,128)(2,1)S(1)} %multiply_reduce_fusion.1), channel_id=1, source_target_pairs={{0,2},{1,3},{2,4},{3,5},{4,6},{5,7},{6,8},{7,9},{8,10},{9,11},{10,... | collective-permute-start | bytes 393224 | tf_op jit(solution)/shard_map/ppermute | solution.py:16
  29.2 7.9 %collective-permute-start.5 = (bf16[256,256]{1,0:T(8,128)(2,1)S(1)}, bf16[256,256]{1,0:T(8,128)(2,1)S(1)}, u32[]{:S(2)}, u32[]{:S(2)}) collective-permute-start(bf16[256,256]{1,0:T(8,128)(2,1)S(1)} %multiply_reduce_fusion.1), channel_id=1, source_target_pairs={{0,1},{1,2},{2,3},{3,4},{4,5},{5,6},{6,7},{7,8},{8,9},{9,10},{10,1... | collective-permute-start | bytes 393224 | tf_op jit(solution)/shard_map/ppermute | solution.py:16
  29.3 7.8 %collective-permute-start.6 = (bf16[256,256]{1,0:T(8,128)(2,1)S(1)}, bf16[256,256]{1,0:T(8,128)(2,1)S(1)}, u32[]{:S(2)}, u32[]{:S(2)}) collective-permute-start(bf16[256,256]{1,0:T(8,128)(2,1)S(1)} %multiply_reduce_fusion.1), channel_id=1, source_target_pairs={{0,127},{1,0},{2,1},{3,2},{4,3},{5,4},{6,5},{7,6},{8,7},{9,8},{10,... | collective-permute-start | bytes 393224 | tf_op jit(solution)/shard_map/ppermute | solution.py:16
  33.4 6.7 %collective-permute-start.7 = (bf16[256,256]{1,0:T(8,128)(2,1)S(1)}, bf16[256,256]{1,0:T(8,128)(2,1)S(1)}, u32[]{:S(2)}, u32[]{:S(2)}) collective-permute-start(bf16[256,256]{1,0:T(8,128)(2,1)S(1)} %multiply_reduce_fusion.1), channel_id=1, source_target_pairs={{0,126},{1,127},{2,0},{3,1},{4,2},{5,3},{6,4},{7,5},{8,6},{9,7},{1... | collective-permute-start | bytes 393224 | tf_op jit(solution)/shard_map/ppermute | solution.py:16
  45.3 199.2 %copy-start = (bf16[4,32,512]{2,1,0:T(8,128)(2,1)}, bf16[4,32,512]{2,1,0:T(8,128)(2,1)S(1)}, u32[]{:S(2)}) copy-start(bf16[4,32,512]{2,1,0:T(8,128)(2,1)S(1)} %reshape.595) | copy-start | bytes 393220
  158.7 43.1 %all-to-all-start = ((bf16[128,2,256]{2,1,0:T(2,128)(2,1)}), bf16[128,2,256]{2,1,0:T(2,128)(2,1)S(1)}, u32[]{:S(2)}, u32[]{:S(2)}) async-start(bf16[128,2,256]{2,1,0:T(2,128)(2,1)} %reshape.624), calls=%async_computation | async-start | bytes 262144 | tf_op jit(solution)/shard_map/all_to_all | solution.py:110
  235.0 9.5 %copy-start.2 = (bf16[4,32,512]{2,1,0:T(8,128)(2,1)S(1)}, bf16[4,32,512]{2,1,0:T(8,128)(2,1)}, u32[]{:S(2)}) copy-start(bf16[4,32,512]{2,1,0:T(8,128)(2,1)} %param.7) | copy-start | bytes 393220
  237.7 18.5 %all-to-all-start.1 = ((bf16[128,2,256]{2,1,0:T(2,128)(2,1)}), bf16[128,2,256]{2,1,0:T(2,128)(2,1)S(1)}, u32[]{:S(2)}, u32[]{:S(2)}) async-start(bf16[128,2,256]{2,1,0:T(2,128)(2,1)} %reshape.626), calls=%async_computation.1 | async-start | bytes 262144 | tf_op jit(solution)/shard_map/all_to_all | solution.py:123
  343.7 27.1 %all-to-all-start.2 = ((bf16[128,3,2,4,128]{4,3,2,1,0:T(4,128)(2,1)}), bf16[128,3,2,4,128]{4,3,2,1,0:T(4,128)(2,1)S(1)}, u32[]{:S(2)}, u32[]{:S(2)}) async-start(bf16[128,3,2,4,128]{4,3,2,1,0:T(4,128)(2,1)} %constant_dynamic-update-slice_fusion.10), calls=%async_computation.2 | async-start | bytes 1572864 | tf_op jit(solution)/shard_map/all_to_all | solution.py:139
  425.7 4.7 %copy-start.1 = (f32[3,4,32,512]{3,2,1,0:T(8,128)S(1)}, f32[3,4,32,512]{3,2,1,0:T(8,128)}, u32[]{:S(2)}) copy-start(f32[3,4,32,512]{3,2,1,0:T(8,128)} %param.8) | copy-start | bytes 2359300
